TPU v7x, 32 devices: a whole 2x2x4 slice. The times are simulated.
32 devices in a mesh: rows: 8 (over z, y), cols: 4 (over x, core).
Axes of the slice: x: 2, y: 2, z: 4, core: 2. Of those that a mesh axis runs over, the one named last changes fastest.
Arguments:
- points: float32 [8192, 1024], P('rows', 'cols'), may hold values from -6 to 6
- pivots: int32 [2, 512], replicated, may hold values from 0 to 8191, as said below
- targets: float32 [8192, 256], P('rows', 'cols'), may hold values from -6 to 6
Outputs:
- factor: float32 [8192, 1024], P(('rows', 'cols'))
- projection: float32 [1024, 256], P(None, 'cols')
Inputs may be any that keep to these rules, and one draw needn't show every extreme that they name: All 1024 indices of both blocks are distinct. The points of one index of rows (an aligned run of 1024 indices) hold at most 512 pivots of the two blocks together, and in every draw some index of rows holds exactly 512.
All inputs are finite; a program needn't handle non-finite values.
Results may differ from a plain program's by a relative error of at most 0.0003.
Values sent between devices are 32-bit elements; how exact they have to be, the bound alone decides.
No kernel may reach another device: no remote copies, remote signals or barrier semaphores. Data moves between devices by JAX's collectives and lax.ppermute only.
A program may use at most 64 MiB of HBM per device.

v0:
```python
import math
import jax
import jax.numpy as jnp
from jax import lax
from jax.sharding import PartitionSpec as P

E = 1024
RIDGE = 0.001


def right_side_solve(low, values):
    return lax.linalg.triangular_solve(low, values, left_side=False, lower=True, transpose_a=True)


def shards(points, pivots, targets):
    highest = lax.Precision.HIGHEST
    rows_dev = points.shape[0]
    nrows = lax.axis_size("rows")
    row_me = lax.axis_index("rows")
    block = pivots.shape[1]
    flat = pivots.reshape(-1)
    owner = flat // rows_dev
    inside = flat - owner * rows_dev
    mine = owner == row_me
    capacity = min(rows_dev, 8 * block // nrows)
    hits = (owner[:, None] == jnp.arange(nrows, dtype=jnp.int32)[None, :]).astype(jnp.int32)
    before = jnp.cumsum(hits, axis=0) - hits
    slot = jnp.sum(before * hits, axis=1)
    place = jnp.where(mine, slot, capacity)
    slot_rows = jnp.zeros((capacity,), jnp.int32).at[place].set(inside, mode="drop")
    picked = points[slot_rows]
    gathered = lax.all_gather(picked, "rows", axis=0, tiled=True)
    pivot_part = gathered[owner * capacity + slot]
    own_rows = lax.all_to_all(points, "cols", split_axis=0, concat_axis=1, tiled=True)
    pivot_full = lax.all_gather(pivot_part, "cols", axis=1, tiled=True)
    own_norms = jnp.sum(own_rows * own_rows, axis=1)
    full_norms = jnp.sum(pivot_full * pivot_full, axis=1)
    cross = jnp.dot(own_rows, pivot_full.T, precision=highest, preferred_element_type=jnp.float32)
    dist = own_norms[:, None] + full_norms[None, :] - 2.0 * cross
    kern = jnp.exp(-dist / (2.0 * E))
    first = kern[:, :block]
    second = kern[:, block:]
    identity = jnp.eye(block, dtype=jnp.float32)
    every_norms = jnp.sum(pivot_full * pivot_full, axis=1)
    pivot_cross = jnp.dot(
        pivot_full, pivot_full.T, precision=highest, preferred_element_type=jnp.float32
    )
    pivot_kern = jnp.exp(
        -(every_norms[:, None] + every_norms[None, :] - 2.0 * pivot_cross) / (2.0 * E)
    )
    low_one = jnp.linalg.cholesky(pivot_kern[:block, :block] + RIDGE * identity)
    factor_one = right_side_solve(low_one, first)
    crossed = right_side_solve(low_one, pivot_kern[block:, :block])
    second_pivot = pivot_kern[block:, block:]
    resid = second - jnp.dot(
        factor_one, crossed.T, precision=highest, preferred_element_type=jnp.float32
    )
    schur = second_pivot - jnp.dot(
        crossed, crossed.T, precision=highest, preferred_element_type=jnp.float32
    )
    low_two = jnp.linalg.cholesky(schur + RIDGE * identity)
    second_lower_matrix = right_side_solve(low_two, resid)
    factor = jnp.concatenate([factor_one, second_lower_matrix], axis=1)
    scaling = 1.0 / math.sqrt(rows_dev * nrows)
    summed = lax.dot_general(
        lax.all_gather(factor, "cols", axis=0, tiled=True),
        targets,
        (((0,), (0,)), ((), ())),
        precision=highest,
        preferred_element_type=jnp.float32,
    )
    projection = lax.psum(summed, "rows") * scaling
    return (factor, projection)


def solution(mesh):
    return jax.shard_map(
        shards,
        mesh=mesh,
        in_specs=(P("rows", "cols"), P(), P("rows", "cols")),
        out_specs=(P(("rows", "cols"), None), P(None, "cols")),
        check_vma=False,
    )
```

profile of v0, /device:TPU:0, one launch (start us, length us, event | category | flops | bytes accessed | tf_op | source)
XLA Modules:
  0.0 580.4 jit_solution(16799073077159931661)
XLA Ops:
  12.3 4.3 scatter_custom_fusion
  16.6 3.5 gather_fusion
  20.1 75.6 %all-gather.8.cloned.1.call-done = f32[4096,256]{1,0:T(8,128)} async-done(((f32[512,256]{1,0:T(8,128)}), f32[4096,256]{1,0:T(8,128)}) %all-gather.8.cloned.1.call-update) | async-done | bytes 4194320 | tf_op jit(solution)/shard_map/all_gather | solution.py:32
  95.8 6.9 %gather_fusion.1 = f32[1024,256]{1,0:T(8,128)} fusion(f32[4096,256]{1,0:T(8,128)} %all-gather.8.cloned.1.call-done, s32[1024]{0:T(1024)S(1)} %broadcast_clamp_fusion), kind=kCustom, calls=%fused_computation.1 | custom fusion | bytes 2101248 | tf_op jit(solution)/shard_map/gather | solution.py:33
  102.7 3.5 all-to-all-start
  106.4 23.6 %all-to-all-done = f32[4,256,256]{2,1,0:T(8,128)S(1)} async-done(((f32[4,256,256]{2,1,0:T(8,128)}), f32[4,256,256]{2,1,0:T(8,128)S(1)}, u32[]{:S(2)}, u32[]{:S(2)}) %all-to-all-start) | async-done | bytes 1048608 | tf_op jit(solution)/shard_map/all_to_all | solution.py:34
  130.5 14.2 %all-gather.10.cloned.1.call-done = f32[1024,1024]{1,0:T(8,128)} async-done(((f32[1024,256]{1,0:T(8,128)}), f32[1024,1024]{1,0:T(8,128)}) %all-gather.10.cloned.1.call-update) | async-done | bytes 4194320 | tf_op jit(solution)/shard_map/all_gather | solution.py:35
  144.7 2.7 multiply_reduce_fusion
  148.1 14.4 %multiply_exponential_fusion = f32[1024,1024]{0,1:T(8,128)S(1)} fusion(f32[1024,1024]{1,0:T(8,128)S(1)} %copy-done.1, f32[1024]{0:T(1024)S(1)} %multiply_reduce_fusion), kind=kOutput, calls=%fused_computation.7 | convolution fusion | flops 12890144768 | bytes 8392704 | tf_op jit(solution)/shard_map/dot_general | solution.py:45
  166.4 11.7 %cholesky.286 = f32[128,128]{1,0:T(8,128)S(1)} custom-call(f32[128,128]{1,0:T(8,128)S(1)} %cholesky.426), custom_call_target="Cholesky" | custom-call | tf_op jit(solution)/shard_map/jit(cholesky)/cholesky | solution.py:51
  178.2 9.8 %custom-call.31 = f32[1,128,128]{1,2,0:T(8,128)S(1)} custom-call(f32[1,128,128]{2,1,0:T(8,128)S(1)} %get-tuple-element.95), custom_call_target="InvertDiagBlocksLowerTriangular" | custom-call | tf_op jit(solution)/shard_map/jit(cholesky)/cholesky | solution.py:51
  188.9 12.1 %cholesky.305 = f32[128,128]{1,0:T(8,128)S(1)} custom-call(f32[128,128]{1,0:T(8,128)S(1)} %cholesky.430), custom_call_target="Cholesky" | custom-call | tf_op jit(solution)/shard_map/jit(cholesky)/cholesky | solution.py:51
  201.1 9.8 %custom-call.32 = f32[1,128,128]{1,2,0:T(8,128)S(1)} custom-call(f32[1,128,128]{2,1,0:T(8,128)S(1)} %get-tuple-element.93), custom_call_target="InvertDiagBlocksLowerTriangular" | custom-call | tf_op jit(solution)/shard_map/jit(cholesky)/cholesky | solution.py:51
  212.9 11.7 %cholesky.326 = f32[128,128]{1,0:T(8,128)S(1)} custom-call(f32[128,128]{1,0:T(8,128)S(1)} %cholesky.435), custom_call_target="Cholesky" | custom-call | tf_op jit(solution)/shard_map/jit(cholesky)/cholesky | solution.py:51
  224.8 9.8 %custom-call.33 = f32[1,128,128]{1,2,0:T(8,128)S(1)} custom-call(f32[1,128,128]{2,1,0:T(8,128)S(1)} %get-tuple-element.91), custom_call_target="InvertDiagBlocksLowerTriangular" | custom-call | tf_op jit(solution)/shard_map/jit(cholesky)/cholesky | solution.py:51
  236.2 11.9 %cholesky.343 = f32[128,128]{1,0:T(8,128)S(1)} custom-call(f32[128,128]{1,0:T(8,128)S(1)} %convolution_subtract_fusion.16), custom_call_target="Cholesky" | custom-call | tf_op jit(solution)/shard_map/jit(cholesky)/cholesky | solution.py:51
  252.9 8.4 %while.5 = (s32[]{:T(128)}, f32[512,512]{0,1:T(8,128)S(1)}, s32[4,2]{0,1:T(2,128)S(1)}, f32[4,128,128]{2,1,0:T(8,128)S(1)}, s32[]{:T(128)}) while((s32[]{:T(128)}, f32[512,512]{0,1:T(8,128)S(1)}, s32[4,2]{0,1:T(2,128)S(1)}, f32[4,128,128]{2,1,0:T(8,128)S(1)}, s32[]{:T(128)}) %tuple.65), condition=%wide.while_cond, body=%wide.while_body.sunk | while | flops 2 | bytes 393329 | solution.py:12
  261.3 39.3 %custom-call.34 = f32[4,128,128]{1,2,0:T(8,128)S(1)} custom-call(f32[4,128,128]{2,1,0:T(8,128)S(1)} %get-tuple-element.26), custom_call_target="InvertDiagBlocksLowerTriangular" | custom-call | tf_op jit(solution)/shard_map/triangular_solve/custom-call.3 | solution.py:12
  302.0 5.5 fusion.4
  315.8 3.1 select_add_fusion
  322.2 12.1 %cholesky.358 = f32[128,128]{1,0:T(8,128)S(1)} custom-call(f32[128,128]{1,0:T(8,128)S(1)} %cholesky.439), custom_call_target="Cholesky" | custom-call | tf_op jit(solution)/shard_map/jit(cholesky)/cholesky | solution.py:61
  335.0 9.8 %custom-call.35 = f32[1,128,128]{1,2,0:T(8,128)S(1)} custom-call(f32[1,128,128]{2,1,0:T(8,128)S(1)} %get-tuple-element.89), custom_call_target="InvertDiagBlocksLowerTriangular" | custom-call | tf_op jit(solution)/shard_map/jit(cholesky)/cholesky | solution.py:61
  345.6 11.7 %cholesky.377 = f32[128,128]{1,0:T(8,128)S(1)} custom-call(f32[128,128]{1,0:T(8,128)S(1)} %cholesky.443), custom_call_target="Cholesky" | custom-call | tf_op jit(solution)/shard_map/jit(cholesky)/cholesky | solution.py:61
  358.1 9.8 %custom-call.36 = f32[1,128,128]{1,2,0:T(8,128)S(1)} custom-call(f32[1,128,128]{2,1,0:T(8,128)S(1)} %get-tuple-element.86), custom_call_target="InvertDiagBlocksLowerTriangular" | custom-call | tf_op jit(solution)/shard_map/jit(cholesky)/cholesky | solution.py:61
  368.6 11.9 %cholesky.398 = f32[128,128]{1,0:T(8,128)S(1)} custom-call(f32[128,128]{1,0:T(8,128)S(1)} %cholesky.448), custom_call_target="Cholesky" | custom-call | tf_op jit(solution)/shard_map/jit(cholesky)/cholesky | solution.py:61
  381.2 9.8 %custom-call.37 = f32[1,128,128]{1,2,0:T(8,128)S(1)} custom-call(f32[1,128,128]{2,1,0:T(8,128)S(1)} %get-tuple-element.83), custom_call_target="InvertDiagBlocksLowerTriangular" | custom-call | tf_op jit(solution)/shard_map/jit(cholesky)/cholesky | solution.py:61
  391.6 11.7 %cholesky.415 = f32[128,128]{1,0:T(8,128)S(1)} custom-call(f32[128,128]{1,0:T(8,128)S(1)} %convolution_subtract_fusion.15), custom_call_target="Cholesky" | custom-call | tf_op jit(solution)/shard_map/jit(cholesky)/cholesky | solution.py:61
  406.7 8.2 %while.6 = (s32[]{:T(128)}, f32[512,512]{1,0:T(8,128)S(1)}, s32[4,2]{0,1:T(2,128)S(1)}, f32[4,128,128]{2,1,0:T(8,128)S(1)}, s32[]{:T(128)}) while((s32[]{:T(128)}, f32[512,512]{1,0:T(8,128)S(1)}, s32[4,2]{0,1:T(2,128)S(1)}, f32[4,128,128]{2,1,0:T(8,128)S(1)}, s32[]{:T(128)}) %tuple.79), condition=%wide.while_cond.clone, body=%wide.while_body.clone.sunk | while | flops 2 | bytes 131189 | solution.py:12
  414.9 39.5 %custom-call.38 = f32[4,128,128]{1,2,0:T(8,128)S(1)} custom-call(f32[4,128,128]{2,1,0:T(8,128)S(1)} %get-tuple-element.27), custom_call_target="InvertDiagBlocksLowerTriangular" | custom-call | tf_op jit(solution)/shard_map/triangular_solve/custom-call.3 | solution.py:12
  461.5 32.2 %all-gather.6.cloned.1.call-done = f32[1024,1024]{0,1:T(8,128)} async-done(((f32[256,1024]{0,1:T(8,128)}), f32[1024,1024]{0,1:T(8,128)}) %all-gather.6.cloned.1.call-update) | async-done | bytes 4194320 | tf_op jit(solution)/shard_map/all_gather | solution.py:66
  493.7 7.0 %fusion.104 = f32[1024,64]{0,1:T(8,128)} fusion(f32[1024,1024]{0,1:T(8,128)} %all-gather.6.cloned.1.call-done, f32[1024,64]{0,1:T(8,128)S(1)} %copy-done), kind=kOutput, calls=%fused_computation.215 | convolution fusion | flops 805306368 | bytes 4718592 | tf_op jit(solution)/shard_map/dot_general | solution.py:65
  502.0 69.9 %all-reduce.3.cloned.1.call-done = f32[1024,64]{0,1:T(8,128)} async-done(((f32[1024,64]{0,1:T(8,128)}), f32[1024,64]{0,1:T(8,128)}) %all-reduce.3.cloned.1.call-update) | async-done | bytes 262160 | tf_op jit(solution)/shard_map/psum | solution.py:72
  (160 shorter events, 61.5 us)
Async XLA Ops:
  7.2 486.5 %copy-start = (f32[1024,64]{0,1:T(8,128)S(1)}, f32[1024,64]{0,1:T(8,128)}, u32[]{:S(2)}) copy-start(f32[1024,64]{0,1:T(8,128)} %param.8) | copy-start | bytes 786436
  7.2 88.6 %all-gather.8.cloned.1.call-start = ((), (), s32[]{:S(2)}) async-start(), calls=%async_computation.3 | async-start | bytes 4718592 | tf_op jit(solution)/shard_map/all_gather | solution.py:32
  20.1 124.6 %all-gather.10.cloned.1.call-start = ((), (), s32[]{:S(2)}) async-start(), calls=%async_computation.4 | async-start | bytes 5242880 | tf_op jit(solution)/shard_map/all_gather | solution.py:35
  102.7 27.3 %all-to-all-start = ((f32[4,256,256]{2,1,0:T(8,128)}), f32[4,256,256]{2,1,0:T(8,128)S(1)}, u32[]{:S(2)}, u32[]{:S(2)}) async-start(f32[4,256,256]{2,1,0:T(8,128)} %bitcast.12), calls=%async_computation | async-start | bytes 2097152 | tf_op jit(solution)/shard_map/all_to_all | solution.py:34
  106.2 387.5 %all-gather.6.cloned.1.call-start = ((), (), s32[]{:S(2)}) async-start(), calls=%async_computation.1 | async-start | bytes 5242880 | tf_op jit(solution)/shard_map/all_gather | solution.py:66
  144.7 3.4 copy-start.1
  162.5 1.9 copy-start.4
  166.4 34.7 %copy-start.3 = (f32[512,512]{1,0:T(8,128)}, f32[512,512]{1,0:T(8,128)S(1)}, u32[]{:S(2)}) copy-start(f32[512,512]{1,0:T(8,128)S(1)} %fusion.6) | copy-start | bytes 3145732
  308.5 10.5 %copy-start.5 = (f32[256,128]{0,1:T(8,128)}, f32[256,128]{0,1:T(8,128)S(1)}, u32[]{:S(2)}) copy-start(f32[256,128]{0,1:T(8,128)S(1)} %fusion.77) | copy-start | bytes 393220
  309.2 9.8 %copy-start.7 = (f32[256,128]{0,1:T(8,128)}, f32[256,128]{0,1:T(8,128)S(1)}, u32[]{:S(2)}) copy-start(f32[256,128]{0,1:T(8,128)S(1)} %fusion.79) | copy-start | bytes 393220
  310.1 8.9 %copy-start.9 = (f32[256,128]{0,1:T(8,128)}, f32[256,128]{0,1:T(8,128)S(1)}, u32[]{:S(2)}) copy-start(f32[256,128]{0,1:T(8,128)S(1)} %fusion.81) | copy-start | bytes 393220
  367.9 92.4 %copy-start.6 = (f32[256,128]{0,1:T(8,128)S(1)}, f32[256,128]{0,1:T(8,128)}, u32[]{:S(2)}) copy-start(f32[256,128]{0,1:T(8,128)} %copy-done.5) | copy-start | bytes 393220
  367.9 92.4 %copy-start.8 = (f32[256,128]{0,1:T(8,128)S(1)}, f32[256,128]{0,1:T(8,128)}, u32[]{:S(2)}) copy-start(f32[256,128]{0,1:T(8,128)} %copy-done.7) | copy-start | bytes 393220
  367.9 92.4 %copy-start.10 = (f32[256,128]{0,1:T(8,128)S(1)}, f32[256,128]{0,1:T(8,128)}, u32[]{:S(2)}) copy-start(f32[256,128]{0,1:T(8,128)} %copy-done.9) | copy-start | bytes 393220
  461.4 39.3 %copy-start.2 = (f32[256,1024]{0,1:T(8,128)S(1)}, f32[256,1024]{0,1:T(8,128)}, u32[]{:S(2)}) copy-start(f32[256,1024]{0,1:T(8,128)} %maximum_maximum_fusion) | copy-start | bytes 3145732
  461.4 110.5 %all-reduce.3.cloned.1.call-start = ((), (), s32[]{:S(2)}) async-start(), calls=%async_computation.2 | async-start | bytes 524288 | tf_op jit(solution)/shard_map/psum | solution.py:72
Sparse Core Ops, SparseCore 0:
  20.2 75.5 all-gather.7
  102.8 41.8 all-gather.9
  461.5 32.0 all-gather.5
  500.8 71.0 all-reduce.2
where the time goes:
time: 584 us; the launch traced here: 580 us
  other arithmetic  248 us (42%)
  waiting for transfers between devices  216 us (37%)
  matrix products  54.1 us (9%)
  local copies, waits for them, and re-layouts  39.3 us (7%)
  between operations  19.8 us (3%)
    another operation x15, other arithmetic, shards(): low_two = jnp.linalg.cholesky(schur + RIDGE * identity)  79.6 us
    another operation x5, other arithmetic, right_side_solve(): lax.linalg.triangular_solve(low, values, left_side=False, lower=True, tra...  79.1 us
    another operation x14, other arithmetic, shards(): low_one = jnp.linalg.cholesky(pivot_kern[:block, :block] + RIDGE * identity)  78.9 us
    all_gather x1, waiting for transfers between devices, shards(): gathered = lax.all_gather(picked, 'rows', axis=0, tiled=True)  75.6 us
    psum x1, waiting for transfers between devices, shards(): projection = lax.psum(summed, 'rows') * scaling  69.9 us
    all_gather x1, waiting for transfers between devices, shards(): lax.all_gather(factor, 'cols', axis=0, tiled=True)  32.2 us
    all_to_all x1, waiting for transfers between devices, shards(): lax.all_to_all(points, 'cols', split_axis=0, concat_axis=1, tiled=True)  23.6 us
    another operation x35, local copies, waits for them, and re-layouts, right_side_solve(): lax.linalg.triangular_solve(low, values, left_side=False, lower=True, tra...  16.4 us
  transfers between devices with their start and end apart: 5, of which 5 were waited for; matrix products, arithmetic and copies ran while one was open for 0% of the time, Pallas kernels for 0%

commit v1 on v0

--- a/solution.py
+++ b/solution.py
@@ -69,7 +69,7 @@
         precision=highest,
         preferred_element_type=jnp.float32,
     )
-    projection = lax.psum(summed, "rows") * scaling
+    projection = jnp.sum(lax.all_gather(summed, "rows"), 0) * scaling
     return (factor, projection)
 
 

time: 584 us -> 564 us (0.966)
  waiting for transfers between devices: 216 us -> 194 us
    psum x1 -> x0, waiting for transfers between devices: 69.9 us -> none  [shards(): projection = lax.psum(summed, 'rows') * scaling]
    all_gather x0 -> x1, waiting for transfers between devices: none -> 47.9 us  [shards(): projection = jnp.sum(lax.all_gather(summed, 'rows'), 0) * scaling]
where the time goes in v1:
time: 564 us; the launch traced here: 561 us
  other arithmetic  247 us (44%)
  waiting for transfers between devices  194 us (34%)
  matrix products  54.1 us (10%)
  local copies, waits for them, and re-layouts  42 us (7%)
  between operations  19.8 us (4%)
    another operation x15, other arithmetic, shards(): low_two = jnp.linalg.cholesky(schur + RIDGE * identity)  79.6 us
    another operation x5, other arithmetic, right_side_solve(): lax.linalg.triangular_solve(low, values, left_side=False, lower=True, tra...  79.1 us
    another operation x14, other arithmetic, shards(): low_one = jnp.linalg.cholesky(pivot_kern[:block, :block] + RIDGE * identity)  78.9 us
    all_gather x1, waiting for transfers between devices, shards(): gathered = lax.all_gather(picked, 'rows', axis=0, tiled=True)  75.6 us
    all_gather x1, waiting for transfers between devices, shards(): projection = jnp.sum(lax.all_gather(summed, 'rows'), 0) * scaling  47.9 us
    all_gather x1, waiting for transfers between devices, shards(): lax.all_gather(factor, 'cols', axis=0, tiled=True)  32.2 us
    all_to_all x1, waiting for transfers between devices, shards(): lax.all_to_all(points, 'cols', split_axis=0, concat_axis=1, tiled=True)  23.6 us
    another operation x35, local copies, waits for them, and re-layouts, right_side_solve(): lax.linalg.triangular_solve(low, values, left_side=False, lower=True, tra...  16.4 us
  transfers between devices with their start and end apart: 5, of which 5 were waited for; matrix products, arithmetic and copies ran while one was open for 0% of the time, Pallas kernels for 0%

profile of v1, /device:TPU:0, one launch (start us, length us, event | category | flops | bytes accessed | tf_op | source)
XLA Modules:
  0.0 560.7 jit_solution(11174036652650207555)
XLA Ops:
  12.3 4.3 scatter_custom_fusion
  16.6 3.5 gather_fusion
  20.1 75.6 %all-gather.10.cloned.1.call-done = f32[4096,256]{1,0:T(8,128)} async-done(((f32[512,256]{1,0:T(8,128)}), f32[4096,256]{1,0:T(8,128)}) %all-gather.10.cloned.1.call-update) | async-done | bytes 4194320 | tf_op jit(solution)/shard_map/all_gather | solution.py:32
  95.8 6.9 %gather_fusion.1 = f32[1024,256]{1,0:T(8,128)} fusion(f32[4096,256]{1,0:T(8,128)} %all-gather.10.cloned.1.call-done, s32[1024]{0:T(1024)S(1)} %broadcast_clamp_fusion), kind=kCustom, calls=%fused_computation.1 | custom fusion | bytes 2101248 | tf_op jit(solution)/shard_map/gather | solution.py:33
  102.7 3.5 all-to-all-start
  106.4 23.6 %all-to-all-done = f32[4,256,256]{2,1,0:T(8,128)S(1)} async-done(((f32[4,256,256]{2,1,0:T(8,128)}), f32[4,256,256]{2,1,0:T(8,128)S(1)}, u32[]{:S(2)}, u32[]{:S(2)}) %all-to-all-start) | async-done | bytes 1048608 | tf_op jit(solution)/shard_map/all_to_all | solution.py:34
  130.5 14.2 %all-gather.12.cloned.1.call-done = f32[1024,1024]{1,0:T(8,128)} async-done(((f32[1024,256]{1,0:T(8,128)}), f32[1024,1024]{1,0:T(8,128)}) %all-gather.12.cloned.1.call-update) | async-done | bytes 4194320 | tf_op jit(solution)/shard_map/all_gather | solution.py:35
  148.1 14.4 %multiply_exponential_fusion = f32[1024,1024]{0,1:T(8,128)S(1)} fusion(f32[1024,1024]{1,0:T(8,128)S(1)} %copy-done.1, f32[1024]{0:T(1024)S(1)} %multiply_reduce_fusion), kind=kOutput, calls=%fused_computation.7 | convolution fusion | flops 12890144768 | bytes 8392704 | tf_op jit(solution)/shard_map/dot_general | solution.py:45
  166.4 11.7 %cholesky.286 = f32[128,128]{1,0:T(8,128)S(1)} custom-call(f32[128,128]{1,0:T(8,128)S(1)} %cholesky.426), custom_call_target="Cholesky" | custom-call | tf_op jit(solution)/shard_map/jit(cholesky)/cholesky | solution.py:51
  178.2 9.8 %custom-call.31 = f32[1,128,128]{1,2,0:T(8,128)S(1)} custom-call(f32[1,128,128]{2,1,0:T(8,128)S(1)} %get-tuple-element.95), custom_call_target="InvertDiagBlocksLowerTriangular" | custom-call | tf_op jit(solution)/shard_map/jit(cholesky)/cholesky | solution.py:51
  188.9 12.1 %cholesky.305 = f32[128,128]{1,0:T(8,128)S(1)} custom-call(f32[128,128]{1,0:T(8,128)S(1)} %cholesky.430), custom_call_target="Cholesky" | custom-call | tf_op jit(solution)/shard_map/jit(cholesky)/cholesky | solution.py:51
  201.1 9.8 %custom-call.32 = f32[1,128,128]{1,2,0:T(8,128)S(1)} custom-call(f32[1,128,128]{2,1,0:T(8,128)S(1)} %get-tuple-element.93), custom_call_target="InvertDiagBlocksLowerTriangular" | custom-call | tf_op jit(solution)/shard_map/jit(cholesky)/cholesky | solution.py:51
  212.9 11.7 %cholesky.326 = f32[128,128]{1,0:T(8,128)S(1)} custom-call(f32[128,128]{1,0:T(8,128)S(1)} %cholesky.435), custom_call_target="Cholesky" | custom-call | tf_op jit(solution)/shard_map/jit(cholesky)/cholesky | solution.py:51
  224.8 9.8 %custom-call.33 = f32[1,128,128]{1,2,0:T(8,128)S(1)} custom-call(f32[1,128,128]{2,1,0:T(8,128)S(1)} %get-tuple-element.91), custom_call_target="InvertDiagBlocksLowerTriangular" | custom-call | tf_op jit(solution)/shard_map/jit(cholesky)/cholesky | solution.py:51
  236.2 11.9 %cholesky.343 = f32[128,128]{1,0:T(8,128)S(1)} custom-call(f32[128,128]{1,0:T(8,128)S(1)} %convolution_subtract_fusion.16), custom_call_target="Cholesky" | custom-call | tf_op jit(solution)/shard_map/jit(cholesky)/cholesky | solution.py:51
  252.9 8.4 %while.5 = (s32[]{:T(128)}, f32[512,512]{0,1:T(8,128)S(1)}, s32[4,2]{0,1:T(2,128)S(1)}, f32[4,128,128]{2,1,0:T(8,128)S(1)}, s32[]{:T(128)}) while((s32[]{:T(128)}, f32[512,512]{0,1:T(8,128)S(1)}, s32[4,2]{0,1:T(2,128)S(1)}, f32[4,128,128]{2,1,0:T(8,128)S(1)}, s32[]{:T(128)}) %tuple.65), condition=%wide.while_cond, body=%wide.while_body.sunk | while | flops 2 | bytes 393329 | solution.py:12
  261.3 39.3 %custom-call.34 = f32[4,128,128]{1,2,0:T(8,128)S(1)} custom-call(f32[4,128,128]{2,1,0:T(8,128)S(1)} %get-tuple-element.26), custom_call_target="InvertDiagBlocksLowerTriangular" | custom-call | tf_op jit(solution)/shard_map/triangular_solve/custom-call.3 | solution.py:12
  302.0 5.5 fusion.4
  315.8 3.1 select_add_fusion
  322.2 12.1 %cholesky.358 = f32[128,128]{1,0:T(8,128)S(1)} custom-call(f32[128,128]{1,0:T(8,128)S(1)} %cholesky.439), custom_call_target="Cholesky" | custom-call | tf_op jit(solution)/shard_map/jit(cholesky)/cholesky | solution.py:61
  335.0 9.8 %custom-call.35 = f32[1,128,128]{1,2,0:T(8,128)S(1)} custom-call(f32[1,128,128]{2,1,0:T(8,128)S(1)} %get-tuple-element.89), custom_call_target="InvertDiagBlocksLowerTriangular" | custom-call | tf_op jit(solution)/shard_map/jit(cholesky)/cholesky | solution.py:61
  345.6 11.7 %cholesky.377 = f32[128,128]{1,0:T(8,128)S(1)} custom-call(f32[128,128]{1,0:T(8,128)S(1)} %cholesky.443), custom_call_target="Cholesky" | custom-call | tf_op jit(solution)/shard_map/jit(cholesky)/cholesky | solution.py:61
  358.1 9.8 %custom-call.36 = f32[1,128,128]{1,2,0:T(8,128)S(1)} custom-call(f32[1,128,128]{2,1,0:T(8,128)S(1)} %get-tuple-element.86), custom_call_target="InvertDiagBlocksLowerTriangular" | custom-call | tf_op jit(solution)/shard_map/jit(cholesky)/cholesky | solution.py:61
  368.6 11.9 %cholesky.398 = f32[128,128]{1,0:T(8,128)S(1)} custom-call(f32[128,128]{1,0:T(8,128)S(1)} %cholesky.448), custom_call_target="Cholesky" | custom-call | tf_op jit(solution)/shard_map/jit(cholesky)/cholesky | solution.py:61
  381.2 9.8 %custom-call.37 = f32[1,128,128]{1,2,0:T(8,128)S(1)} custom-call(f32[1,128,128]{2,1,0:T(8,128)S(1)} %get-tuple-element.83), custom_call_target="InvertDiagBlocksLowerTriangular" | custom-call | tf_op jit(solution)/shard_map/jit(cholesky)/cholesky | solution.py:61
  391.6 11.7 %cholesky.415 = f32[128,128]{1,0:T(8,128)S(1)} custom-call(f32[128,128]{1,0:T(8,128)S(1)} %convolution_subtract_fusion.15), custom_call_target="Cholesky" | custom-call | tf_op jit(solution)/shard_map/jit(cholesky)/cholesky | solution.py:61
  406.7 8.2 %while.6 = (s32[]{:T(128)}, f32[512,512]{1,0:T(8,128)S(1)}, s32[4,2]{0,1:T(2,128)S(1)}, f32[4,128,128]{2,1,0:T(8,128)S(1)}, s32[]{:T(128)}) while((s32[]{:T(128)}, f32[512,512]{1,0:T(8,128)S(1)}, s32[4,2]{0,1:T(2,128)S(1)}, f32[4,128,128]{2,1,0:T(8,128)S(1)}, s32[]{:T(128)}) %tuple.79), condition=%wide.while_cond.clone, body=%wide.while_body.clone.sunk | while | flops 2 | bytes 131189 | solution.py:12
  414.9 39.5 %custom-call.38 = f32[4,128,128]{1,2,0:T(8,128)S(1)} custom-call(f32[4,128,128]{2,1,0:T(8,128)S(1)} %get-tuple-element.27), custom_call_target="InvertDiagBlocksLowerTriangular" | custom-call | tf_op jit(solution)/shard_map/triangular_solve/custom-call.3 | solution.py:12
  461.5 32.2 %all-gather.8.cloned.1.call-done = f32[1024,1024]{0,1:T(8,128)} async-done(((f32[256,1024]{0,1:T(8,128)}), f32[1024,1024]{0,1:T(8,128)}) %all-gather.8.cloned.1.call-update) | async-done | bytes 4194320 | tf_op jit(solution)/shard_map/all_gather | solution.py:66
  493.7 7.0 %fusion.104 = f32[1024,64]{0,1:T(8,128)} fusion(f32[1024,1024]{0,1:T(8,128)} %all-gather.8.cloned.1.call-done, f32[1024,64]{0,1:T(8,128)S(1)} %copy-done), kind=kOutput, calls=%fused_computation.216 | convolution fusion | flops 805306368 | bytes 4718592 | tf_op jit(solution)/shard_map/dot_general | solution.py:65
  502.0 47.9 %all-gather.14.cloned.1.call-done = f32[8192,64]{0,1:T(8,128)} async-done(((f32[1024,64]{0,1:T(8,128)}), f32[8192,64]{0,1:T(8,128)}) %all-gather.14.cloned.1.call-update) | async-done | bytes 2097168 | tf_op jit(solution)/shard_map/all_gather | solution.py:72
  549.9 2.8 copy.78
  (162 shorter events, 63.8 us)
Async XLA Ops:
  7.2 486.5 %copy-start = (f32[1024,64]{0,1:T(8,128)S(1)}, f32[1024,64]{0,1:T(8,128)}, u32[]{:S(2)}) copy-start(f32[1024,64]{0,1:T(8,128)} %param.8) | copy-start | bytes 786436
  7.2 88.6 %all-gather.10.cloned.1.call-start = ((), (), s32[]{:S(2)}) async-start(), calls=%async_computation.2 | async-start | bytes 4718592 | tf_op jit(solution)/shard_map/all_gather | solution.py:32
  20.1 124.6 %all-gather.12.cloned.1.call-start = ((), (), s32[]{:S(2)}) async-start(), calls=%async_computation.3 | async-start | bytes 5242880 | tf_op jit(solution)/shard_map/all_gather | solution.py:35
  102.7 27.3 %all-to-all-start = ((f32[4,256,256]{2,1,0:T(8,128)}), f32[4,256,256]{2,1,0:T(8,128)S(1)}, u32[]{:S(2)}, u32[]{:S(2)}) async-start(f32[4,256,256]{2,1,0:T(8,128)} %bitcast.12), calls=%async_computation | async-start | bytes 2097152 | tf_op jit(solution)/shard_map/all_to_all | solution.py:34
  106.2 387.5 %all-gather.8.cloned.1.call-start = ((), (), s32[]{:S(2)}) async-start(), calls=%async_computation.1 | async-start | bytes 5242880 | tf_op jit(solution)/shard_map/all_gather | solution.py:66
  144.7 3.4 copy-start.1
  162.5 1.9 copy-start.4
  166.4 34.7 %copy-start.3 = (f32[512,512]{1,0:T(8,128)}, f32[512,512]{1,0:T(8,128)S(1)}, u32[]{:S(2)}) copy-start(f32[512,512]{1,0:T(8,128)S(1)} %fusion.6) | copy-start | bytes 3145732
  308.5 10.5 %copy-start.5 = (f32[256,128]{0,1:T(8,128)}, f32[256,128]{0,1:T(8,128)S(1)}, u32[]{:S(2)}) copy-start(f32[256,128]{0,1:T(8,128)S(1)} %fusion.77) | copy-start | bytes 393220
  309.2 9.8 %copy-start.7 = (f32[256,128]{0,1:T(8,128)}, f32[256,128]{0,1:T(8,128)S(1)}, u32[]{:S(2)}) copy-start(f32[256,128]{0,1:T(8,128)S(1)} %fusion.79) | copy-start | bytes 393220
  310.1 8.9 %copy-start.9 = (f32[256,128]{0,1:T(8,128)}, f32[256,128]{0,1:T(8,128)S(1)}, u32[]{:S(2)}) copy-start(f32[256,128]{0,1:T(8,128)S(1)} %fusion.81) | copy-start | bytes 393220
  367.9 92.4 %copy-start.6 = (f32[256,128]{0,1:T(8,128)S(1)}, f32[256,128]{0,1:T(8,128)}, u32[]{:S(2)}) copy-start(f32[256,128]{0,1:T(8,128)} %copy-done.5) | copy-start | bytes 393220
  367.9 92.4 %copy-start.8 = (f32[256,128]{0,1:T(8,128)S(1)}, f32[256,128]{0,1:T(8,128)}, u32[]{:S(2)}) copy-start(f32[256,128]{0,1:T(8,128)} %copy-done.7) | copy-start | bytes 393220
  367.9 92.4 %copy-start.10 = (f32[256,128]{0,1:T(8,128)S(1)}, f32[256,128]{0,1:T(8,128)}, u32[]{:S(2)}) copy-start(f32[256,128]{0,1:T(8,128)} %copy-done.9) | copy-start | bytes 393220
  461.4 39.3 %copy-start.2 = (f32[256,1024]{0,1:T(8,128)S(1)}, f32[256,1024]{0,1:T(8,128)}, u32[]{:S(2)}) copy-start(f32[256,1024]{0,1:T(8,128)} %maximum_maximum_fusion) | copy-start | bytes 3145732
  461.4 88.5 %all-gather.14.cloned.1.call-start = ((), (), s32[]{:S(2)}) async-start(), calls=%async_computation.4 | async-start | bytes 2359296 | tf_op jit(solution)/shard_map/all_gather | solution.py:72
Sparse Core Ops, SparseCore 0:
  20.2 75.5 all-gather.9
  102.8 41.8 all-gather.11
  461.5 32.0 all-gather.7
  500.8 49.0 all-gather.13
